TPU v7x, 512 devices: a whole 4x4x16 slice. The times are simulated.
512 devices in a mesh: attn: 8 (over y, core), exp: 16 (over z), seq: 4 (over x).
Axes of the slice: x: 4, y: 4, z: 16, core: 2. Of those that a mesh axis runs over, the one named last changes fastest.
Arguments:
- tokens: bfloat16 [256, 6144], P(('attn', 'exp'), 'seq'), may hold values from -6 to 6
- modality: int32 [256], P(('attn', 'exp')), may hold values from 0 to 1, as said below
- cotangent: bfloat16 [256, 6144], P(('attn', 'exp'), 'seq'), may hold values from -6 to 6
- gate_speech: bfloat16 [6144, 24576], P('seq', ('attn', 'exp')), may hold values from -0.078125 to 0.078125
- up_speech: bfloat16 [6144, 24576], P('seq', ('attn', 'exp')), may hold values from -0.078125 to 0.078125
- down_speech: bfloat16 [24576, 6144], P(('attn', 'exp'), 'seq'), may hold values from -0.078125 to 0.078125
- gate_text: bfloat16 [6144, 16384], P('seq', ('attn', 'exp')), may hold values from -0.078125 to 0.078125
- up_text: bfloat16 [6144, 16384], P('seq', ('attn', 'exp')), may hold values from -0.078125 to 0.078125
- down_text: bfloat16 [16384, 6144], P(('attn', 'exp'), 'seq'), may hold values from -0.09375 to 0.09375
Outputs:
- mixed: bfloat16 [256, 6144], P(('attn', 'exp'), 'seq')
- token_grad: bfloat16 [256, 6144], P(('attn', 'exp'), 'seq')
- down_speech_grad: bfloat16 [24576, 6144], P(('attn', 'exp'), 'seq')
- down_text_grad: bfloat16 [16384, 6144], P(('attn', 'exp'), 'seq')
Inputs may be any that keep to these rules, and one draw needn't show every extreme that they name: Exactly 160 tokens of the window have modality 0 and the other 96 have modality 1, at places drawn from the seed.
All inputs are finite; a program needn't handle non-finite values.
Results may differ from a plain program's by a relative error of at most 0.005.
Values may be sent and summed in bfloat16 or wider, within the bound.
A program may use at most 64 MiB of HBM per device.

v0:
```python
import jax
import jax.numpy as jnp
from jax import lax
from jax.sharding import PartitionSpec as P


def contract_first(left, right):
    return lax.dot_general(
        left, right, (((0,), (0,)), ((), ())), preferred_element_type=jnp.float32
    )


def contract_last(left, right):
    return lax.dot_general(
        left, right, (((1,), (1,)), ((), ())), preferred_element_type=jnp.float32
    )


def shards(
    tokens, modality, cotangent, gate_speech, up_speech, down_speech, gate_text, up_text, down_text
):
    rows, grads, kinds = (
        lax.all_gather(tokens, ("attn", "exp"), axis=0, tiled=True),
        lax.all_gather(cotangent, ("attn", "exp"), axis=0, tiled=True),
        lax.all_gather(modality, ("attn", "exp"), axis=0, tiled=True),
    )
    speech = (kinds == 0)[:, None]
    features = lax.all_gather(rows, "seq", axis=1, tiled=True)
    full_gs, full_us, full_gt, full_ut = (
        lax.all_gather(gate_speech, "seq", axis=0, tiled=True),
        lax.all_gather(up_speech, "seq", axis=0, tiled=True),
        lax.all_gather(gate_text, "seq", axis=0, tiled=True),
        lax.all_gather(up_text, "seq", axis=0, tiled=True),
    )
    zero = jnp.zeros_like(grads)
    speech_grads = jnp.where(speech, grads, zero)
    text_grads = jnp.where(speech, zero, grads)
    terms = (
        jnp.dot(features, full_gs, preferred_element_type=jnp.float32),
        jnp.dot(features, full_us, preferred_element_type=jnp.float32),
        jnp.dot(features, full_gt, preferred_element_type=jnp.float32),
        jnp.dot(features, full_ut, preferred_element_type=jnp.float32),
    )
    gs, us, gt, ut = terms
    hs = (jax.nn.silu(gs) * us).astype(jnp.bfloat16)
    ht = (jax.nn.silu(gt) * ut).astype(jnp.bfloat16)
    speech_out = jnp.dot(hs, down_speech, preferred_element_type=jnp.float32)
    text_out = jnp.dot(ht, down_text, preferred_element_type=jnp.float32)
    partial_out = jnp.where(speech, speech_out, text_out)
    mixed = lax.psum_scatter(partial_out, ("attn", "exp"), scatter_dimension=0, tiled=True).astype(
        jnp.bfloat16
    )
    dhs, dht = lax.psum(
        (contract_last(speech_grads, down_speech), contract_last(text_grads, down_text)), "seq"
    )
    sig_s = jax.nn.sigmoid(gs)
    sig_t = jax.nn.sigmoid(gt)
    dgs = (dhs * us * sig_s * (1.0 + gs * (1.0 - sig_s))).astype(jnp.bfloat16)
    dus = (dhs * jax.nn.silu(gs)).astype(jnp.bfloat16)
    dgt = (dht * ut * sig_t * (1.0 + gt * (1.0 - sig_t))).astype(jnp.bfloat16)
    dut = (dht * jax.nn.silu(gt)).astype(jnp.bfloat16)
    speech_back = contract_last(dgs, gate_speech) + contract_last(dus, up_speech)
    text_back = contract_last(dgt, gate_text) + contract_last(dut, up_text)
    partial_grad = speech_back + text_back
    token_grad = lax.psum_scatter(
        partial_grad, ("attn", "exp"), scatter_dimension=0, tiled=True
    ).astype(jnp.bfloat16)
    down_speech_grad = contract_first(hs, speech_grads).astype(jnp.bfloat16)
    down_text_grad = contract_first(ht, text_grads).astype(jnp.bfloat16)
    return (mixed, token_grad, down_speech_grad, down_text_grad)


def solution(mesh):
    return jax.shard_map(
        shards,
        mesh=mesh,
        in_specs=(
            P(("attn", "exp"), "seq"),
            P(("attn", "exp")),
            P(("attn", "exp"), "seq"),
            P("seq", ("attn", "exp")),
            P("seq", ("attn", "exp")),
            P(("attn", "exp"), "seq"),
            P("seq", ("attn", "exp")),
            P("seq", ("attn", "exp")),
            P(("attn", "exp"), "seq"),
        ),
        out_specs=(
            P(("attn", "exp"), "seq"),
            P(("attn", "exp"), "seq"),
            P(("attn", "exp"), "seq"),
            P(("attn", "exp"), "seq"),
        ),
        check_vma=False,
    )
```

profile of v0, /device:TPU:2, one launch (start us, length us, event | category | flops | bytes accessed | tf_op | source)
XLA Modules:
  0.0 866.6 jit_solution(7845797920021915052)
XLA Ops:
  7.2 0.7 all-gather.10.cloned.1.call-update
  8.0 100.8 %all-gather = bf16[128,2,1536]{2,1,0:T(2,128)(2,1)S(1)} all-gather(bf16[1,2,1536]{2,1,0:T(2,128)(2,1)} %bitcast.24), channel_id=1, replica_groups=mesh['attn'=8,'exp'=16,'seq'=4] {'attn','exp'}, dimensions={0}, use_global_device_ids=true | all-gather | bytes 792576 | tf_op jit(solution)/shard_map/all_gather | solution.py:23
  108.8 1.2 reshape.13
  110.0 0.7 all-gather.12.cloned.1.call-update
  111.4 0.5 all-gather.16.cloned.1.call-update
  112.0 92.1 %all-gather.1 = bf16[128,2,1536]{2,1,0:T(2,128)(2,1)S(1)} all-gather(bf16[1,2,1536]{2,1,0:T(2,128)(2,1)S(1)} %bitcast.25), channel_id=1, replica_groups=mesh['attn'=8,'exp'=16,'seq'=4] {'attn','exp'}, dimensions={0}, use_global_device_ids=true | all-gather | bytes 792576 | tf_op jit(solution)/shard_map/all_gather | solution.py:24
  204.4 0.7 fusion.19
  206.1 23.4 %all-reduce = s32[256]{0:T(256)S(1)} all-reduce(s32[256]{0:T(256)S(1)} %dynamic-update-slice), channel_id=1, replica_groups=mesh['attn'=8,'exp'=16,'seq'=4] {'attn','exp'}, use_global_device_ids=true, to_apply=%add | all-reduce | flops 256 | bytes 2048
  229.5 1.1 fusion.2
  230.6 1.2 fusion.1
  232.5 3.8 fusion.20
  236.3 4.6 multiply_convert_fusion.2
  240.9 1.6 fusion.21
  242.4 3.3 fusion.22
  245.8 20.4 %all-gather.16.cloned.1.call-done = bf16[6144,128]{1,0:T(8,128)(2,1)} async-done(((bf16[1536,128]{1,0:T(8,128)(2,1)}), bf16[6144,128]{1,0:T(8,128)(2,1)}) %all-gather.16.cloned.1.call-update) | async-done | bytes 1572880 | tf_op jit(solution)/shard_map/all_gather | solution.py:33
  266.2 4.1 multiply_convert_fusion.5
  270.6 0.8 copy-done.10
  271.4 1.1 convolution_convert_fusion.1
  272.5 1.2 convolution_convert_fusion
  273.7 52.4 %all-reduce.8.cloned.1.call-done = (f32[256,192]{0,1:T(8,128)}, f32[256,128]{1,0:T(8,128)}) async-done(((f32[256,192]{0,1:T(8,128)}, f32[256,128]{1,0:T(8,128)}), (f32[256,192]{0,1:T(8,128)}, f32[256,128]{1,0:T(8,128)})) %all-reduce.8.cloned.1.call-update) | async-done | bytes 327696 | tf_op jit(solution)/shard_map/psum | solution.py:53
  326.1 1.6 fusion.5
  329.3 1.6 fusion
  330.8 527.6 %all-reduce.9 = (bf16[256,1536]{1,0:T(8,128)(2,1)S(1)}, bf16[256,1536]{1,0:T(8,128)(2,1)}) all-reduce(f32[256,1536]{1,0:T(8,128)S(1)} %convolution_select_fusion, f32[256,1536]{1,0:T(8,128)} %fusion), channel_id=2, replica_groups=mesh['attn'=8,'exp'=16,'seq'=4] {'attn','exp'}, use_global_device_ids=true, to_apply=%region_0.1.clone | all-reduce | flops 786432 | bytes 4718592
  858.4 1.3 dynamic-slice_convert_fusion
  (53 shorter events, 3.3 us)
Async XLA Ops:
  7.2 223.4 %copy-start = (bf16[192,1536]{1,0:T(8,128)(2,1)S(1)}, bf16[192,1536]{1,0:T(8,128)(2,1)}, u32[]{:S(2)}) copy-start(bf16[192,1536]{1,0:T(8,128)(2,1)} %param.14) | copy-start | bytes 1769476
  7.2 225.3 %all-gather.10.cloned.1.call-start = ((), (), s32[]{:S(2)}) async-start(), calls=%async_computation.1 | async-start | bytes 2949120 | tf_op jit(solution)/shard_map/all_gather | solution.py:30
  7.9 224.5 %all-gather.8.cloned.1.call-start = ((), (), s32[]{:S(2)}) async-start(), calls=%async_computation | async-start | bytes 3932160 | tf_op jit(solution)/shard_map/all_gather | solution.py:28
  108.8 3.2 copy-start.14
  110.0 126.3 %all-gather.12.cloned.1.call-start = ((), (), s32[]{:S(2)}) async-start(), calls=%async_computation.2 | async-start | bytes 2949120 | tf_op jit(solution)/shard_map/all_gather | solution.py:31
  110.7 93.7 %copy-start.15 = (u32[512]{0:T(512)S(1)}, u32[512]{0:T(512)}, u32[]{:S(2)}) copy-start(u32[512]{0:T(512)} %constant.21) | copy-start | bytes 6148
  110.8 95.1 %copy-start.16 = (s32[2]{0:T(128)S(1)}, s32[2]{0:T(128)}, u32[]{:S(2)}) copy-start(s32[2]{0:T(128)} %param.10) | copy-start | bytes 28
  110.8 118.7 %copy-start.13 = (bf16[128,1536]{1,0:T(8,128)(2,1)S(1)}, bf16[128,1536]{1,0:T(8,128)(2,1)}, u32[]{:S(2)}) copy-start(bf16[128,1536]{1,0:T(8,128)(2,1)} %param.17) | copy-start | bytes 1179652
  110.8 131.7 %all-gather.14.cloned.1.call-start = ((), (), s32[]{:S(2)}) async-start(), calls=%async_computation.3 | async-start | bytes 1966080 | tf_op jit(solution)/shard_map/all_gather | solution.py:32
  111.4 154.8 %all-gather.16.cloned.1.call-start = ((), (), s32[]{:S(2)}) async-start(), calls=%async_computation.4 | async-start | bytes 1966080 | tf_op jit(solution)/shard_map/all_gather | solution.py:33
  111.9 214.2 %all-reduce.8.cloned.1.call-start = ((), (), s32[]{:S(2)}) async-start(), calls=%async_computation.5 | async-start | bytes 655360 | tf_op jit(solution)/shard_map/psum | solution.py:53
  204.4 27.3 %copy-start.9 = (bf16[256,1536]{1,0:T(8,128)(2,1)}, bf16[256,1536]{1,0:T(8,128)(2,1)S(1)}, u32[]{:S(2)}) copy-start(bf16[256,1536]{1,0:T(8,128)(2,1)S(1)} %reshape.15) | copy-start | bytes 2359300
  236.3 4.6 copy-start.4
  266.2 4.1 copy-start.1
  270.3 1.1 copy-start.10
  271.4 54.7 %copy-start.2 = (bf16[1536,192]{0,1:T(8,128)(2,1)S(1)}, bf16[1536,192]{0,1:T(8,128)(2,1)}, u32[]{:S(2)}) copy-start(bf16[1536,192]{0,1:T(8,128)(2,1)} %param.12) | copy-start | bytes 1769476
  273.7 54.0 %copy-start.3 = (bf16[1536,192]{0,1:T(8,128)(2,1)S(1)}, bf16[1536,192]{0,1:T(8,128)(2,1)}, u32[]{:S(2)}) copy-start(bf16[1536,192]{0,1:T(8,128)(2,1)} %param.13) | copy-start | bytes 1769476
  326.1 1.6 copy-start.5
  326.1 1.6 copy-start.8
  327.7 1.0 copy-start.6
  327.8 1.0 copy-start.11
  327.8 1.1 copy-start.12
  328.2 1.1 copy-start.7
Sparse Core Ops, SparseCore 0:
  10.1 44.2 all-gather.9
  110.1 40.5 all-gather.7
  152.8 40.8 all-gather.11
  195.6 34.1 all-gather.13
  231.8 34.3 all-gather.15
  268.4 57.6 all-reduce.7
where the time goes:
time: 867 us
  blocking collectives  744 us (86%)
  waiting for transfers between devices  75.3 us (9%)
  matrix products  26.2 us (3%)
  between operations  15.7 us (2%)
    unnamed x2, blocking collectives  551 us
    all_gather x1, blocking collectives, shards(): lax.all_gather(tokens, ('attn', 'exp'), axis=0, tiled=True)  101 us
    all_gather x1, blocking collectives, shards(): lax.all_gather(cotangent, ('attn', 'exp'), axis=0, tiled=True)  92.1 us
    psum x1, waiting for transfers between devices, shards(): lax.psum((contract_last(speech_grads, down_speech), contract_last(text_gr...  52.4 us
    all_gather x1, waiting for transfers between devices, shards(): lax.all_gather(up_text, 'seq', axis=0, tiled=True)  20.4 us
  transfers between devices with their start and end apart: 6, of which 2 were waited for; matrix products, arithmetic and copies ran while one was open for 3% of the time, Pallas kernels for 0%

commit v1 on v0

--- a/solution.py
+++ b/solution.py
@@ -2,6 +2,18 @@
 import jax.numpy as jnp
 from jax import lax
 from jax.sharding import PartitionSpec as P
+
+
+def build_the_threads(vector):
+    return jnp.concatenate(
+        lax.all_to_all(
+            jnp.stack([vector for _ in range(lax.axis_size(("attn", "exp")))], axis=0),
+            ("attn", "exp"),
+            split_axis=0,
+            concat_axis=0,
+        ),
+        axis=0,
+    )
 
 
 def contract_first(left, right):
@@ -20,7 +32,7 @@
     tokens, modality, cotangent, gate_speech, up_speech, down_speech, gate_text, up_text, down_text
 ):
     rows, grads, kinds = (
-        lax.all_gather(tokens, ("attn", "exp"), axis=0, tiled=True),
+        build_the_threads(tokens),
         lax.all_gather(cotangent, ("attn", "exp"), axis=0, tiled=True),
         lax.all_gather(modality, ("attn", "exp"), axis=0, tiled=True),
     )

time: 867 us -> 829 us (0.956)
  the two profiles are of different devices: /device:TPU:2 before, /device:TPU:6 now
where the time goes in v1:
time: 829 us; the launch traced here: 828 us
  blocking collectives  707 us (85%)
  waiting for transfers between devices  72.4 us (9%)
  matrix products  26.1 us (3%)
  between operations  15.7 us (2%)
    unnamed x2, blocking collectives  551 us
    all_gather x1, blocking collectives, shards(): lax.all_gather(cotangent, ('attn', 'exp'), axis=0, tiled=True)  94 us
    all_to_all x1, blocking collectives, build_the_threads(): lax.all_to_all(jnp.stack([vector for _ in range(lax.axis_size(('attn', 'e...  62.1 us
    psum x1, waiting for transfers between devices, shards(): lax.psum((contract_last(speech_grads, down_speech), contract_last(text_gr...  52.3 us
    all_gather x1, waiting for transfers between devices, shards(): lax.all_gather(up_text, 'seq', axis=0, tiled=True)  17.6 us
  transfers between devices with their start and end apart: 6, of which 2 were waited for; matrix products, arithmetic and copies ran while one was open for 3% of the time, Pallas kernels for 0%

profile of v1, /device:TPU:6, one launch (start us, length us, event | category | flops | bytes accessed | tf_op | source)
XLA Modules:
  0.0 828.2 jit_solution(17185344658421393670)
XLA Ops:
  7.2 0.7 all-gather.9.cloned.1.call-update
  8.0 1.1 stack.2
  9.1 62.1 %all_to_all.5 = bf16[128,2,1536]{2,1,0:T(2,128)(2,1)S(1)} all-to-all(bf16[128,2,1536]{2,1,0:T(2,128)(2,1)S(1)} %stack.2), channel_id=1, replica_groups=mesh['attn'=8,'exp'=16,'seq'=4] {'attn','exp'}, dimensions={0} | all-to-all | bytes 1572864 | tf_op jit(solution)/shard_map/all_to_all | solution.py:9
  71.2 1.2 reshape.14
  72.4 0.7 all-gather.11.cloned.1.call-update
  74.4 94.0 %all-gather = bf16[128,2,1536]{2,1,0:T(2,128)(2,1)S(1)} all-gather(bf16[1,2,1536]{2,1,0:T(2,128)(2,1)S(1)} %bitcast.23), channel_id=1, replica_groups=mesh['attn'=8,'exp'=16,'seq'=4] {'attn','exp'}, dimensions={0}, use_global_device_ids=true | all-gather | bytes 792576 | tf_op jit(solution)/shard_map/all_gather | solution.py:36
  168.7 0.7 fusion.19
  170.4 23.5 %all-reduce = s32[256]{0:T(256)S(1)} all-reduce(s32[256]{0:T(256)S(1)} %dynamic-update-slice), channel_id=1, replica_groups=mesh['attn'=8,'exp'=16,'seq'=4] {'attn','exp'}, use_global_device_ids=true, to_apply=%add | all-reduce | flops 256 | bytes 2048
  193.8 1.1 fusion.2
  194.9 1.2 fusion.1
  196.8 3.8 fusion.20
  200.6 4.6 multiply_convert_fusion.2
  205.2 1.6 fusion.21
  206.8 3.3 fusion.22
  210.1 17.6 %all-gather.15.cloned.1.call-done = bf16[6144,128]{1,0:T(8,128)(2,1)} async-done(((bf16[1536,128]{1,0:T(8,128)(2,1)}), bf16[6144,128]{1,0:T(8,128)(2,1)}) %all-gather.15.cloned.1.call-update) | async-done | bytes 1572880 | tf_op jit(solution)/shard_map/all_gather | solution.py:45
  227.7 4.1 multiply_convert_fusion.5
  232.1 0.8 copy-done.10
  232.9 1.1 convolution_convert_fusion.1
  234.0 1.2 convolution_convert_fusion
  235.2 52.3 %all-reduce.8.cloned.1.call-done = (f32[256,192]{0,1:T(8,128)}, f32[256,128]{1,0:T(8,128)}) async-done(((f32[256,192]{0,1:T(8,128)}, f32[256,128]{1,0:T(8,128)}), (f32[256,192]{0,1:T(8,128)}, f32[256,128]{1,0:T(8,128)})) %all-reduce.8.cloned.1.call-update) | async-done | bytes 327696 | tf_op jit(solution)/shard_map/psum | solution.py:65
  287.5 1.6 fusion.5
  290.6 1.6 fusion
  292.2 527.8 %all-reduce.9 = (bf16[256,1536]{1,0:T(8,128)(2,1)S(1)}, bf16[256,1536]{1,0:T(8,128)(2,1)}) all-reduce(f32[256,1536]{1,0:T(8,128)S(1)} %convolution_select_fusion, f32[256,1536]{1,0:T(8,128)} %fusion), channel_id=2, replica_groups=mesh['attn'=8,'exp'=16,'seq'=4] {'attn','exp'}, use_global_device_ids=true, to_apply=%region_0.1.clone | all-reduce | flops 786432 | bytes 4718592
  820.0 1.3 dynamic-slice_convert_fusion
  (54 shorter events, 3.8 us)
Async XLA Ops:
  7.2 187.7 %copy-start = (bf16[192,1536]{1,0:T(8,128)(2,1)S(1)}, bf16[192,1536]{1,0:T(8,128)(2,1)}, u32[]{:S(2)}) copy-start(bf16[192,1536]{1,0:T(8,128)(2,1)} %param.14) | copy-start | bytes 1769476
  7.2 189.6 %all-gather.9.cloned.1.call-start = ((), (), s32[]{:S(2)}) async-start(), calls=%async_computation.2 | async-start | bytes 2949120 | tf_op jit(solution)/shard_map/all_gather | solution.py:42
  7.9 188.9 %all-gather.7.cloned.1.call-start = ((), (), s32[]{:S(2)}) async-start(), calls=%async_computation.1 | async-start | bytes 3932160 | tf_op jit(solution)/shard_map/all_gather | solution.py:40
  71.2 3.2 copy-start.14
  72.4 128.2 %all-gather.11.cloned.1.call-start = ((), (), s32[]{:S(2)}) async-start(), calls=%async_computation.3 | async-start | bytes 2949120 | tf_op jit(solution)/shard_map/all_gather | solution.py:43
  73.1 95.6 %copy-start.15 = (u32[512]{0:T(512)S(1)}, u32[512]{0:T(512)}, u32[]{:S(2)}) copy-start(u32[512]{0:T(512)} %constant.21) | copy-start | bytes 6148
  73.1 97.0 %copy-start.16 = (s32[2]{0:T(128)S(1)}, s32[2]{0:T(128)}, u32[]{:S(2)}) copy-start(s32[2]{0:T(128)} %param.10) | copy-start | bytes 28
  73.2 120.7 %copy-start.13 = (bf16[128,1536]{1,0:T(8,128)(2,1)S(1)}, bf16[128,1536]{1,0:T(8,128)(2,1)}, u32[]{:S(2)}) copy-start(bf16[128,1536]{1,0:T(8,128)(2,1)} %param.17) | copy-start | bytes 1179652
  73.2 133.6 %all-gather.13.cloned.1.call-start = ((), (), s32[]{:S(2)}) async-start(), calls=%async_computation.4 | async-start | bytes 1966080 | tf_op jit(solution)/shard_map/all_gather | solution.py:44
  73.7 153.9 %all-gather.15.cloned.1.call-start = ((), (), s32[]{:S(2)}) async-start(), calls=%async_computation.5 | async-start | bytes 1966080 | tf_op jit(solution)/shard_map/all_gather | solution.py:45
  74.3 213.2 %all-reduce.8.cloned.1.call-start = ((), (), s32[]{:S(2)}) async-start(), calls=%async_computation.6 | async-start | bytes 655360 | tf_op jit(solution)/shard_map/psum | solution.py:65
  168.7 27.3 %copy-start.9 = (bf16[256,1536]{1,0:T(8,128)(2,1)}, bf16[256,1536]{1,0:T(8,128)(2,1)S(1)}, u32[]{:S(2)}) copy-start(bf16[256,1536]{1,0:T(8,128)(2,1)S(1)} %reshape.19) | copy-start | bytes 2359300
  200.6 4.6 copy-start.4
  227.7 4.1 copy-start.1
  231.8 1.1 copy-start.10
  232.9 54.6 %copy-start.2 = (bf16[1536,192]{0,1:T(8,128)(2,1)S(1)}, bf16[1536,192]{0,1:T(8,128)(2,1)}, u32[]{:S(2)}) copy-start(bf16[1536,192]{0,1:T(8,128)(2,1)} %param.12) | copy-start | bytes 1769476
  235.2 53.9 %copy-start.3 = (bf16[1536,192]{0,1:T(8,128)(2,1)S(1)}, bf16[1536,192]{0,1:T(8,128)(2,1)}, u32[]{:S(2)}) copy-start(bf16[1536,192]{0,1:T(8,128)(2,1)} %param.13) | copy-start | bytes 1769476
  287.5 1.6 copy-start.5
  287.5 1.6 copy-start.8
  289.1 1.0 copy-start.6
  289.1 1.0 copy-start.11
  289.1 1.1 copy-start.12
  289.6 1.1 copy-start.7
Sparse Core Ops, SparseCore 0:
  10.1 43.2 all-gather.8
  72.5 38.6 all-gather.6
  113.3 40.9 all-gather.10
  156.2 35.1 all-gather.12
  193.3 34.3 all-gather.14
  229.9 57.5 all-reduce.7
